TPU v7x, 32 devices: a whole 2x2x4 slice. The times are simulated.
32 devices in a mesh: dp: 8 (over y, x, core), tensor: 4 (over z).
Axes of the slice: x: 2, y: 2, z: 4, core: 2. Of those that a mesh axis runs over, the one named last changes fastest.
Arguments:
- hidden: bfloat16 [1536, 16384], P('dp', 'tensor'), may hold values from -6 to 6
- cotangent: bfloat16 [1536, 16384], P('dp', 'tensor'), may hold values from -6 to 6
- blocks: bfloat16 [7, 64, 256, 256], P(None, 'tensor', 'dp'), may hold values from -0.125 to 0.125
- low_left: bfloat16 [16384, 128], P('tensor'), may hold values from -0.046875 to 0.046875
- low_right: bfloat16 [128, 16384], P(None, 'tensor'), may hold values from -0.5 to 0.5
Outputs:
- mixed_rows: bfloat16 [1536, 16384], P('dp', 'tensor')
- grad_hidden: bfloat16 [1536, 16384], P('dp', 'tensor')
- grad_blocks: float32 [7, 64, 256, 256], P(None, 'tensor', 'dp')
- grad_left: float32 [16384, 128], P('tensor')
- grad_right: float32 [128, 16384], P(None, 'tensor')
All inputs are finite; a program needn't handle non-finite values.
Results may differ from a plain program's by a relative error of at most 0.0095.
Values may be sent and summed in bfloat16 or wider, within the bound.
No kernel may reach another device: no remote copies, remote signals or barrier semaphores. Data moves between devices by JAX's collectives and lax.ppermute only.
A program may use at most 256 MiB of HBM per device.

v0:
```python
import jax
import jax.numpy as jnp
from jax import lax
from jax.sharding import PartitionSpec as P


def partner(value, axis, bit):
    return lax.ppermute(value, axis, [(i, i ^ 1 << bit) for i in range(lax.axis_size(axis))])


def flip_blocks(values, distance):
    array_shape = values.shape
    grouped = values.reshape(
        array_shape[:-2] + (array_shape[-2] // (2 * distance), 2, distance, array_shape[-1])
    )
    return grouped[..., ::-1, :, :].reshape(array_shape)


def per_device(hidden, cotangent, blocks, low_left, low_right):
    tok_rows, ff_local = hidden.shape
    blocks_here = blocks.shape[1]
    block_size = blocks.shape[3]
    local_bits = blocks_here.bit_length() - 1
    cross_bits = lax.axis_size("tensor").bit_length() - 1
    grad_scale = jnp.float32(1.0) / jnp.sqrt(jnp.float32(tok_rows * lax.axis_size("dp")))
    weights = lax.all_gather(blocks, "dp", axis=2, tiled=True)
    inputs_b = hidden.reshape(tok_rows, blocks_here, block_size)
    local_inputs = [inputs_b] + [
        flip_blocks(inputs_b, 2**level_idx) for level_idx in range(local_bits)
    ]
    remote_inputs = [partner(inputs_b, "tensor", bit_idx) for bit_idx in range(cross_bits)]
    stacked_in = jnp.stack(local_inputs + remote_inputs)
    mixed_blocks = jnp.einsum(
        "ktnb,knbc->tnc", stacked_in, weights, preferred_element_type=jnp.float32
    )
    partial_in = jnp.dot(hidden, low_left, preferred_element_type=jnp.float32)
    factor_b = lax.psum(partial_in, "tensor").astype(jnp.bfloat16)
    low_term = jnp.dot(factor_b, low_right, preferred_element_type=jnp.float32)
    mixed_rows = (mixed_blocks.reshape(tok_rows, ff_local) + low_term).astype(jnp.bfloat16)
    cot_b = cotangent.reshape(tok_rows, blocks_here, block_size)
    block_terms = (
        jnp.einsum("ktnb,tnc->knbc", stacked_in, cot_b, preferred_element_type=jnp.float32)
        * grad_scale
    )
    grad_blocks = lax.psum_scatter(
        block_terms.astype(jnp.bfloat16), "dp", scatter_dimension=2, tiled=True
    ).astype(jnp.float32)
    products = jnp.einsum("tnc,knbc->ktnb", cot_b, weights, preferred_element_type=jnp.float32)
    grad_in = products[0]
    for level_idx in range(local_bits):
        grad_in = grad_in + flip_blocks(products[1 + level_idx], 2**level_idx)
    for bit_idx in range(cross_bits):
        sent_terms = products[1 + local_bits + bit_idx]
        grad_in = grad_in + partner(sent_terms, "tensor", bit_idx)
    partial_back = jnp.einsum("tf,rf->tr", cotangent, low_right, preferred_element_type=jnp.float32)
    back_b = lax.psum(partial_back, "tensor").astype(jnp.bfloat16)
    low_back = jnp.einsum("tr,fr->tf", back_b, low_left, preferred_element_type=jnp.float32)
    grad_hidden = (grad_in.reshape(tok_rows, ff_local) + low_back).astype(jnp.bfloat16)
    part_left = (
        jnp.einsum("tf,tr->fr", hidden, back_b, preferred_element_type=jnp.float32) * grad_scale
    )
    part_right = (
        jnp.einsum("tr,tf->rf", factor_b, cotangent, preferred_element_type=jnp.float32)
        * grad_scale
    )
    grad_left, grad_right = lax.psum((part_left, part_right), "dp")
    return (mixed_rows, grad_hidden, grad_blocks, grad_left, grad_right)


def solution(mesh):
    placed = (
        P("dp", "tensor"),
        P("dp", "tensor"),
        P(None, "tensor", "dp", None),
        P("tensor", None),
        P(None, "tensor"),
    )
    return jax.shard_map(
        per_device,
        mesh=mesh,
        in_specs=placed,
        out_specs=(
            P("dp", "tensor"),
            P("dp", "tensor"),
            P(None, "tensor", "dp", None),
            P("tensor", None),
            P(None, "tensor"),
        ),
        check_vma=False,
    )
```

profile of v0, /device:TPU:0, one launch (start us, length us, event | category | flops | bytes accessed | tf_op | source)
XLA Modules:
  0.0 353.8 jit_solution(5965905838084927043)
XLA Ops:
  7.2 3.0 copy.29
  11.7 4.1 %collective-permute-start.1 = (bf16[192,16,256]{2,0,1:T(8,128)(2,1)}, bf16[192,16,256]{2,0,1:T(8,128)(2,1)}, u32[]{:S(2)}, u32[]{:S(2)}) collective-permute-start(bf16[192,16,256]{2,0,1:T(8,128)(2,1)} %bitcast.91), channel_id=1, source_target_pairs={{0,2},{1,3},{2,0},{3,1},{4,6},{5,7},{6,4},{7,5},{8,10},{9,11},{10,... | collective-permute-start | bytes 4718600 | tf_op jit(solution)/shard_map/ppermute | solution.py:8
  18.4 82.4 %all-reduce.6 = (bf16[192,128]{1,0:T(8,128)(2,1)S(1)}, bf16[192,128]{1,0:T(8,128)(2,1)S(1)}) all-reduce(f32[192,128]{1,0:T(8,128)S(1)} %fusion.18, f32[192,128]{1,0:T(8,128)S(1)} %fusion.19), channel_id=1, replica_groups=mesh['dp'=8,'tensor'=4] {'tensor'}, use_global_device_ids=true, to_apply=%region_0.0 | all-reduce | flops 49152 | bytes 294912 | tf_op jit(solution)/shard_map/psum | solution.py:37
  100.9 3.2 convolution_multiply_fusion
  104.1 1.8 fusion.2
  106.1 2.4 reshape_reshape.14
  108.5 2.4 reshape_reshape.13
  110.9 2.4 reshape_reshape.12
  116.7 3.2 copy.24
  119.9 2.8 rev.26
  124.4 2.7 rev.25
  127.1 3.3 copy.22
  130.3 2.7 rev.24
  133.0 1.7 copy_dynamic-update-slice_fusion
  140.3 2.8 bitcast_dynamic-update-slice_fusion.1
  143.1 2.7 bitcast_dynamic-update-slice_fusion
  145.8 11.5 %fusion = bf16[7,16,256,256]{3,2,0,1:T(8,128)(2,1)} fusion(bf16[7,192,16,256]{3,1,0,2:T(8,128)(2,1)} %bitcast_dynamic-update-slice_fusion, bf16[192,16,256,1]{2,1,0,3:T(8,128)(2,1)S(1)} %bitcast.103), kind=kOutput, calls=%fused_computation.1 | convolution fusion | flops 2833252352 | bytes 27262976 | tf_op jit(solution)/shard_map/ktnb,tnc->knbc/dot_general | solution.py:42
  157.4 13.9 %convolution_bitcast_fusion = f32[7,192,16,256]{3,1,0,2:T(8,128)} fusion(bf16[7,16,256,256]{3,2,0,1:T(8,128)(2,1)} %all-gather.2.cloned.1.call-done, bf16[192,16,256,1]{2,1,0,3:T(8,128)(2,1)S(1)} %bitcast.104), kind=kOutput, calls=%fused_computation.2 | convolution fusion | flops 2818572288 | bytes 38273024 | tf_op jit(solution)/shard_map/tnc,knbc->ktnb/dot_general | solution.py:48
  171.2 13.8 %fusion.17 = (f32[1,192,16,256]{3,1,0,2:T(8,128)}, f32[192,16,256]{2,0,1:T(8,128)}, f32[1,192,16,256]{3,1,0,2:T(8,128)}, f32[1,192,16,256]{3,1,0,2:T(8,128)}, f3...) fusion(f32[7,192,16,256]{3,1,0,2:T(8,128)} %convolution_bitcast_fusion), kind=kLoop, calls=%fused_computation.35 | loop fusion | bytes 37748736 | tf_op jit(solution)/shard_map/slice | solution.py:51
  185.8 2.2 fusion.20
  188.1 2.9 copy.37
  190.9 102.4 %reduce-scatter.2.cloned.1.call-done = bf16[7,16,32,256]{3,2,0,1:T(8,128)(2,1)} async-done(((bf16[7,16,256,256]{3,2,0,1:T(8,128)(2,1)}), bf16[7,16,32,256]{3,2,0,1:T(8,128)(2,1)}) %reduce-scatter.2.cloned.1.call-update) | async-done | bytes 1835024 | tf_op jit(solution)/shard_map/reduce_scatter | solution.py:45
  293.3 3.8 %copy.36 = f32[7,16,32,256]{3,2,1,0:T(8,128)} copy(bf16[7,16,32,256]{3,2,0,1:T(8,128)(2,1)} %reduce-scatter.2.cloned.1.call-done) | data formatting | bytes 5505024
  297.1 12.5 %convolution_bitcast_fusion.1 = f32[16,24,8,256]{3,2,1,0:T(8,128)S(1)} fusion(bf16[7,192,16,256]{3,1,0,2:T(8,128)(2,1)} %bitcast_dynamic-update-slice_fusion, bf16[7,16,256,256]{3,2,0,1:T(8,128)(2,1)} %all-gather.2.cloned.1.call-done), kind=kOutput, calls=%fused_computation.19 | convolution fusion | flops 2818572288 | bytes 28835840 | tf_op jit(solution)/shard_map/ktnb,knbc->tnc/dot_general | solution.py:33
  309.6 2.1 copy.48
  311.7 3.8 %rev.28 = f32[192,8,2,1,256]{4,0,2,1,3:T(8,128)} reverse(f32[192,8,2,1,256]{4,0,2,1,3:T(8,128)} %bitcast.100), dimensions={2} | reverse | bytes 6291456 | tf_op jit(solution)/shard_map/rev | solution.py:16
  315.5 3.9 %rev.31 = f32[192,1,2,8,256]{4,0,3,2,1:T(8,128)} reverse(f32[192,1,2,8,256]{4,0,3,2,1:T(8,128)} %bitcast.99), dimensions={2} | reverse | bytes 6291456 | tf_op jit(solution)/shard_map/rev | solution.py:16
  319.3 3.9 %rev.30 = f32[192,2,2,4,256]{4,0,3,2,1:T(8,128)} reverse(f32[192,2,2,4,256]{4,0,3,2,1:T(8,128)} %bitcast.98), dimensions={2} | reverse | bytes 6291456 | tf_op jit(solution)/shard_map/rev | solution.py:16
  323.2 4.0 %rev.29 = f32[192,4,2,2,256]{4,0,3,2,1:T(8,128)} reverse(f32[192,4,2,2,256]{4,0,3,2,1:T(8,128)} %bitcast.97), dimensions={2} | reverse | bytes 6291456 | tf_op jit(solution)/shard_map/rev | solution.py:16
  327.2 3.7 %fusion.1 = bf16[192,4096]{1,0:T(8,128)(2,1)} fusion(f32[192,4096]{1,0:T(8,128)} %bitcast.101, bf16[128,4096]{1,0:T(8,128)(2,1)S(1)} %copy-done.14, bf16[192,128]{1,0:T(8,128)(2,1)S(1)} %get-tuple-element.17), kind=kOutput, calls=%fused_computation.4 | convolution fusion | flops 202899456 | bytes 5816320 | tf_op jit(solution)/shard_map/dot_general | solution.py:38
  331.0 10.0 %fusion.9 = f32[16,24,8,256]{3,2,1,0:T(8,128)} fusion(f32[192,16,256]{2,0,1:T(8,128)} %collective-permute-done.3, f32[192,16,256]{2,0,1:T(8,128)} %collective-permute-done.2, f32[7,192,16,256]{3,1,0,2:T(8,128)} %convolution_bitcast_fusion, f32[192,1,2,8,256]{4,0,3,2,1:T(8,128)} %rev.31, f32[192,2,2,4,256]{4,0,3,2,1:T(8,128)} %rev.30, ...), kind=kLoop, calls=%fused_computation.17 | loop fusion | flops 4718592 | bytes 25165824
  340.9 2.4 copy.49
  (61 shorter events, 19.8 us)
Async XLA Ops:
  7.2 10.1 %copy-start = (bf16[4096,128]{1,0:T(8,128)(2,1)S(1)}, bf16[4096,128]{1,0:T(8,128)(2,1)}, u32[]{:S(2)}) copy-start(bf16[4096,128]{1,0:T(8,128)(2,1)} %param.8) | copy-start | bytes 3145732
  7.2 3.2 copy-start.1
  7.2 150.2 %all-gather.2.cloned.1.call-start = ((), (), s32[]{:S(2)}) async-start(), calls=%async_computation.1 | async-start | bytes 16515072 | tf_op jit(solution)/shard_map/all_gather | solution.py:26
  10.3 177.8 %all-reduce.5.cloned.1.call-start = ((), (), s32[]{:S(2)}) async-start(), calls=%async_computation.3 | async-start | bytes 8388608 | tf_op jit(solution)/shard_map/psum | solution.py:66
  10.3 7.5 %copy-start.2 = (bf16[192,4096]{1,0:T(8,128)(2,1)S(1)}, bf16[192,4096]{1,0:T(8,128)(2,1)}, u32[]{:S(2)}) copy-start(bf16[192,4096]{1,0:T(8,128)(2,1)} %param.6) | copy-start | bytes 4718596
  10.4 7.5 %copy-start.13 = (bf16[128,4096]{1,0:T(8,128)(2,1)S(1)}, bf16[128,4096]{1,0:T(8,128)(2,1)}, u32[]{:S(2)}) copy-start(bf16[128,4096]{1,0:T(8,128)(2,1)} %param.9) | copy-start | bytes 3145732
  11.7 131.4 %collective-permute-start.1 = (bf16[192,16,256]{2,0,1:T(8,128)(2,1)}, bf16[192,16,256]{2,0,1:T(8,128)(2,1)}, u32[]{:S(2)}, u32[]{:S(2)}) collective-permute-start(bf16[192,16,256]{2,0,1:T(8,128)(2,1)} %bitcast.91), channel_id=1, source_target_pairs={{0,2},{1,3},{2,0},{3,1},{4,6},{5,7},{6,4},{7,5},{8,10},{9,11},{10,... | collective-permute-start | bytes 4718600 | tf_op jit(solution)/shard_map/ppermute | solution.py:8
  15.7 124.6 %collective-permute-start = (bf16[192,16,256]{2,0,1:T(8,128)(2,1)}, bf16[192,16,256]{2,0,1:T(8,128)(2,1)}, u32[]{:S(2)}, u32[]{:S(2)}) collective-permute-start(bf16[192,16,256]{2,0,1:T(8,128)(2,1)} %bitcast.91), channel_id=1, source_target_pairs={{0,1},{1,0},{2,3},{3,2},{4,5},{5,4},{6,7},{7,6},{8,9},{9,8},{10,11... | collective-permute-start | bytes 4718600 | tf_op jit(solution)/shard_map/ppermute | solution.py:8
  105.9 187.4 %reduce-scatter.2.cloned.1.call-start = ((), (), s32[]{:S(2)}) async-start(), calls=%async_computation.2 | async-start | bytes 16515072 | tf_op jit(solution)/shard_map/reduce_scatter | solution.py:45
  113.7 1.1 copy-start.4
  116.7 6.0 %copy-start.11 = (bf16[192,4,2,2,256]{4,3,2,1,0:T(2,128)(2,1)S(1)}, bf16[192,4,2,2,256]{4,3,2,1,0:T(2,128)(2,1)}, u32[]{:S(2)}) copy-start(bf16[192,4,2,2,256]{4,3,2,1,0:T(2,128)(2,1)} %reshape_reshape.13) | copy-start | bytes 4718596
  127.1 6.0 %copy-start.5 = (bf16[24,8,16,256]{3,2,1,0:T(8,128)(2,1)S(1)}, bf16[24,8,16,256]{3,2,1,0:T(8,128)(2,1)}, u32[]{:S(2)}) copy-start(bf16[24,8,16,256]{3,2,1,0:T(8,128)(2,1)} %copy-done.4) | copy-start | bytes 4718596
  133.0 1.7 copy-start.12
  133.0 3.0 copy-start.10
  134.7 2.5 copy-start.9
  136.0 2.5 copy-start.8
  137.3 2.6 copy-start.3
  185.0 146.0 %collective-permute-start.3 = (f32[192,16,256]{2,0,1:T(8,128)}, f32[192,16,256]{2,0,1:T(8,128)}, u32[]{:S(2)}, u32[]{:S(2)}) collective-permute-start(f32[192,16,256]{2,0,1:T(8,128)} %get-tuple-element.20), channel_id=1, source_target_pairs={{0,2},{1,3},{2,0},{3,1},{4,6},{5,7},{6,4},{7,5},{8,10},{9,11},{10,... | collective-permute-start | bytes 9437192 | tf_op jit(solution)/shard_map/ppermute | solution.py:8
  185.8 145.1 %collective-permute-start.2 = (f32[192,16,256]{2,0,1:T(8,128)}, f32[192,16,256]{2,0,1:T(8,128)}, u32[]{:S(2)}, u32[]{:S(2)}) collective-permute-start(f32[192,16,256]{2,0,1:T(8,128)} %get-tuple-element.24), channel_id=1, source_target_pairs={{0,1},{1,0},{2,3},{3,2},{4,5},{5,4},{6,7},{7,6},{8,9},{9,8},{10,11... | collective-permute-start | bytes 9437192 | tf_op jit(solution)/shard_map/ppermute | solution.py:8
  323.2 4.0 %copy-start.14 = (bf16[128,4096]{1,0:T(8,128)(2,1)S(1)}, bf16[128,4096]{1,0:T(8,128)(2,1)}, u32[]{:S(2)}) copy-start(bf16[128,4096]{1,0:T(8,128)(2,1)} %param.9) | copy-start | bytes 3145732
  327.2 3.8 %copy-start.6 = (f32[192,8,2,1,256]{4,0,2,1,3:T(8,128)S(1)}, f32[192,8,2,1,256]{4,0,2,1,3:T(8,128)}, u32[]{:S(2)}) copy-start(f32[192,8,2,1,256]{4,0,2,1,3:T(8,128)} %rev.28) | copy-start | bytes 9437188
  340.9 2.8 copy-start.7
  343.8 2.2 copy-start.15
Sparse Core Ops, SparseCore 0:
  10.5 83.6 all-gather.1
  106.0 79.6 all-reduce.4
  189.7 103.6 reduce-scatter.1
where the time goes:
time: 354 us
  waiting for transfers between devices  102 us (29%)
  local copies, waits for them, and re-layouts  86.7 us (24%)
  blocking collectives  82.4 us (23%)
  matrix products  50 us (14%)
  between operations  13.9 us (4%)
  other arithmetic  11.5 us (3%)
  starting transfers between devices  6.77 us (2%)
    reduce_scatter x1, waiting for transfers between devices, per_device(): lax.psum_scatter(block_terms.astype(jnp.bfloat16), 'dp', scatter_dimensio...  102 us
    psum x1, blocking collectives, per_device(): factor_b = lax.psum(partial_in, 'tensor').astype(jnp.bfloat16)  82.4 us
    rev x8, local copies, waits for them, and re-layouts, flip_blocks(): return grouped[..., ::-1, :, :].reshape(array_shape)  24.9 us
    unnamed x44, local copies, waits for them, and re-layouts  23.7 us
    another operation x7, local copies, waits for them, and re-layouts, flip_blocks(): values.reshape(array_shape[:-2] + (array_shape[-2] // (2 * distance), 2,...  15.8 us
    dot_general x1, matrix products, per_device(): jnp.einsum('tnc,knbc->ktnb', cot_b, weights, preferred_element_type=jnp.f...  13.9 us
    slice x1, local copies, waits for them, and re-layouts, per_device(): grad_in = grad_in + flip_blocks(products[1 + level_idx], 2 ** level_idx)  13.8 us
    dot_general x1, matrix products, per_device(): jnp.einsum('ktnb,knbc->tnc', stacked_in, weights, preferred_element_type=...  12.5 us
  transfers between devices with their start and end apart: 7, of which 1 were waited for; matrix products, arithmetic and copies ran while one was open for 36% of the time, Pallas kernels for 0%

commit v1 on v0

--- a/solution.py
+++ b/solution.py
@@ -34,7 +34,7 @@
         "ktnb,knbc->tnc", stacked_in, weights, preferred_element_type=jnp.float32
     )
     partial_in = jnp.dot(hidden, low_left, preferred_element_type=jnp.float32)
-    factor_b = lax.psum(partial_in, "tensor").astype(jnp.bfloat16)
+    factor_b = jnp.sum(lax.all_gather(partial_in, "tensor"), axis=0).astype(jnp.bfloat16)
     low_term = jnp.dot(factor_b, low_right, preferred_element_type=jnp.float32)
     mixed_rows = (mixed_blocks.reshape(tok_rows, ff_local) + low_term).astype(jnp.bfloat16)
     cot_b = cotangent.reshape(tok_rows, blocks_here, block_size)

time: 354 us -> 369 us (1.042)
  blocking collectives: 82.4 us -> 97.1 us
    all_gather x0 -> x1, blocking collectives: none -> 77 us  [per_device(): lax.all_gather(partial_in, 'tensor')]
    psum x1, blocking collectives: 82.4 us -> 20.2 us  [per_device(): back_b = lax.psum(partial_back, 'tensor').astype(jnp.bfloat16)]
  transfers between devices with their start and end apart: 7 -> 7, of which waited for: 1 -> 1; matrix products, arithmetic and copies ran while one was open for 36% -> 35% of each run, Pallas kernels for 0% -> 0%
where the time goes in v1:
time: 369 us; the launch traced here: 368 us
  waiting for transfers between devices  102 us (28%)
  blocking collectives  97.1 us (26%)
  local copies, waits for them, and re-layouts  86.8 us (24%)
  matrix products  50.2 us (14%)
  between operations  13.9 us (4%)
  other arithmetic  11.5 us (3%)
  starting transfers between devices  6.58 us (2%)
    reduce_scatter x1, waiting for transfers between devices, per_device(): lax.psum_scatter(block_terms.astype(jnp.bfloat16), 'dp', scatter_dimensio...  102 us
    all_gather x1, blocking collectives, per_device(): lax.all_gather(partial_in, 'tensor')  77 us
    rev x8, local copies, waits for them, and re-layouts, flip_blocks(): return grouped[..., ::-1, :, :].reshape(array_shape)  24.9 us
    unnamed x44, local copies, waits for them, and re-layouts  23.7 us
    psum x1, blocking collectives, per_device(): back_b = lax.psum(partial_back, 'tensor').astype(jnp.bfloat16)  20.2 us
    another operation x7, local copies, waits for them, and re-layouts, flip_blocks(): values.reshape(array_shape[:-2] + (array_shape[-2] // (2 * distance), 2,...  15.9 us
    dot_general x1, matrix products, per_device(): jnp.einsum('tnc,knbc->ktnb', cot_b, weights, preferred_element_type=jnp.f...  13.9 us
    slice x1, local copies, waits for them, and re-layouts, per_device(): grad_in = grad_in + flip_blocks(products[1 + level_idx], 2 ** level_idx)  13.8 us
  transfers between devices with their start and end apart: 7, of which 1 were waited for; matrix products, arithmetic and copies ran while one was open for 35% of the time, Pallas kernels for 0%

profile of v1, /device:TPU:0, one launch (start us, length us, event | category | flops | bytes accessed | tf_op | source)
XLA Modules:
  0.0 368.4 jit_solution(2973268063444798598)
XLA Ops:
  7.2 3.0 copy.29
  11.7 4.0 %collective-permute-start.1 = (bf16[192,16,256]{2,0,1:T(8,128)(2,1)}, bf16[192,16,256]{2,0,1:T(8,128)(2,1)}, u32[]{:S(2)}, u32[]{:S(2)}) collective-permute-start(bf16[192,16,256]{2,0,1:T(8,128)(2,1)} %bitcast.92), channel_id=1, source_target_pairs={{0,2},{1,3},{2,0},{3,1},{4,6},{5,7},{6,4},{7,5},{8,10},{9,11},{10,... | collective-permute-start | bytes 4718600 | tf_op jit(solution)/shard_map/ppermute | solution.py:8
  17.8 77.0 %all-gather = f32[768,128]{1,0:T(8,128)S(1)} all-gather(f32[192,128]{1,0:T(8,128)S(1)} %fusion.18), channel_id=2, replica_groups=mesh['dp'=8,'tensor'=4] {'tensor'}, dimensions={0}, use_global_device_ids=true | all-gather | bytes 491520 | tf_op jit(solution)/shard_map/all_gather | solution.py:37
  94.9 3.3 convolution_multiply_fusion
  98.8 20.2 %psum.21 = bf16[192,128]{1,0:T(8,128)(2,1)S(1)} all-reduce(f32[192,128]{1,0:T(8,128)S(1)} %fusion.19), channel_id=1, replica_groups=mesh['dp'=8,'tensor'=4] {'tensor'}, use_global_device_ids=true, to_apply=%region_1.0 | all-reduce | flops 24576 | bytes 147456 | tf_op jit(solution)/shard_map/psum | solution.py:56
  119.0 1.8 fusion.2
  121.0 2.4 reshape_reshape.14
  123.4 2.4 reshape_reshape.13
  125.8 2.4 reshape_reshape.12
  131.6 3.3 copy.24
  134.9 2.7 rev.26
  139.3 2.7 rev.25
  142.0 3.2 copy.22
  145.2 2.7 rev.24
  155.2 2.7 bitcast_dynamic-update-slice_fusion.1
  158.0 2.7 bitcast_dynamic-update-slice_fusion
  160.7 11.5 %fusion = bf16[7,16,256,256]{3,2,0,1:T(8,128)(2,1)} fusion(bf16[7,192,16,256]{3,1,0,2:T(8,128)(2,1)} %bitcast_dynamic-update-slice_fusion, bf16[192,16,256,1]{2,1,0,3:T(8,128)(2,1)S(1)} %bitcast.104), kind=kOutput, calls=%fused_computation.1 | convolution fusion | flops 2833252352 | bytes 27262976 | tf_op jit(solution)/shard_map/ktnb,tnc->knbc/dot_general | solution.py:42
  172.2 13.9 %convolution_bitcast_fusion = f32[7,192,16,256]{3,1,0,2:T(8,128)} fusion(bf16[7,16,256,256]{3,2,0,1:T(8,128)(2,1)} %all-gather.3.cloned.1.call-done, bf16[192,16,256,1]{2,1,0,3:T(8,128)(2,1)S(1)} %bitcast.105), kind=kOutput, calls=%fused_computation.2 | convolution fusion | flops 2818572288 | bytes 38273024 | tf_op jit(solution)/shard_map/tnc,knbc->ktnb/dot_general | solution.py:48
  186.1 13.8 %fusion.17 = (f32[1,192,16,256]{3,1,0,2:T(8,128)}, f32[192,16,256]{2,0,1:T(8,128)}, f32[1,192,16,256]{3,1,0,2:T(8,128)}, f32[1,192,16,256]{3,1,0,2:T(8,128)}, f3...) fusion(f32[7,192,16,256]{3,1,0,2:T(8,128)} %convolution_bitcast_fusion), kind=kLoop, calls=%fused_computation.35 | loop fusion | bytes 37748736 | tf_op jit(solution)/shard_map/slice | solution.py:51
  200.6 2.2 fusion.20
  202.8 2.9 copy.37
  205.7 102.2 %reduce-scatter.2.cloned.1.call-done = bf16[7,16,32,256]{3,2,0,1:T(8,128)(2,1)} async-done(((bf16[7,16,256,256]{3,2,0,1:T(8,128)(2,1)}), bf16[7,16,32,256]{3,2,0,1:T(8,128)(2,1)}) %reduce-scatter.2.cloned.1.call-update) | async-done | bytes 1835024 | tf_op jit(solution)/shard_map/reduce_scatter | solution.py:45
  307.9 3.8 %copy.36 = f32[7,16,32,256]{3,2,1,0:T(8,128)} copy(bf16[7,16,32,256]{3,2,0,1:T(8,128)(2,1)} %reduce-scatter.2.cloned.1.call-done) | data formatting | bytes 5505024
  311.6 12.5 %convolution_bitcast_fusion.1 = f32[16,24,8,256]{3,2,1,0:T(8,128)S(1)} fusion(bf16[7,192,16,256]{3,1,0,2:T(8,128)(2,1)} %bitcast_dynamic-update-slice_fusion, bf16[7,16,256,256]{3,2,0,1:T(8,128)(2,1)} %all-gather.3.cloned.1.call-done), kind=kOutput, calls=%fused_computation.19 | convolution fusion | flops 2818572288 | bytes 28835840 | tf_op jit(solution)/shard_map/ktnb,knbc->tnc/dot_general | solution.py:33
  324.2 2.1 copy.48
  326.3 3.8 %rev.28 = f32[192,8,2,1,256]{4,0,2,1,3:T(8,128)} reverse(f32[192,8,2,1,256]{4,0,2,1,3:T(8,128)} %bitcast.101), dimensions={2} | reverse | bytes 6291456 | tf_op jit(solution)/shard_map/rev | solution.py:16
  330.1 3.8 %rev.31 = f32[192,1,2,8,256]{4,0,3,2,1:T(8,128)} reverse(f32[192,1,2,8,256]{4,0,3,2,1:T(8,128)} %bitcast.100), dimensions={2} | reverse | bytes 6291456 | tf_op jit(solution)/shard_map/rev | solution.py:16
  333.9 3.9 %rev.30 = f32[192,2,2,4,256]{4,0,3,2,1:T(8,128)} reverse(f32[192,2,2,4,256]{4,0,3,2,1:T(8,128)} %bitcast.99), dimensions={2} | reverse | bytes 6291456 | tf_op jit(solution)/shard_map/rev | solution.py:16
  337.8 4.0 %rev.29 = f32[192,4,2,2,256]{4,0,3,2,1:T(8,128)} reverse(f32[192,4,2,2,256]{4,0,3,2,1:T(8,128)} %bitcast.98), dimensions={2} | reverse | bytes 6291456 | tf_op jit(solution)/shard_map/rev | solution.py:16
  341.8 3.7 %fusion.1 = bf16[192,4096]{1,0:T(8,128)(2,1)} fusion(f32[192,4096]{1,0:T(8,128)} %bitcast.102, bf16[128,4096]{1,0:T(8,128)(2,1)S(1)} %copy-done.14, bf16[192,128]{1,0:T(8,128)(2,1)S(1)} %reduce_sum.9), kind=kOutput, calls=%fused_computation.4 | convolution fusion | flops 202899456 | bytes 5816320 | tf_op jit(solution)/shard_map/dot_general | solution.py:38
  345.5 10.0 %fusion.9 = f32[16,24,8,256]{3,2,1,0:T(8,128)} fusion(f32[192,16,256]{2,0,1:T(8,128)} %collective-permute-done.3, f32[192,16,256]{2,0,1:T(8,128)} %collective-permute-done.2, f32[7,192,16,256]{3,1,0,2:T(8,128)} %convolution_bitcast_fusion, f32[192,1,2,8,256]{4,0,3,2,1:T(8,128)} %rev.31, f32[192,2,2,4,256]{4,0,3,2,1:T(8,128)} %rev.30, ...), kind=kLoop, calls=%fused_computation.17 | loop fusion | flops 4718592 | bytes 25165824
  355.5 2.4 copy.49
  (63 shorter events, 21.4 us)
Async XLA Ops:
  7.2 10.1 %copy-start = (bf16[4096,128]{1,0:T(8,128)(2,1)S(1)}, bf16[4096,128]{1,0:T(8,128)(2,1)}, u32[]{:S(2)}) copy-start(bf16[4096,128]{1,0:T(8,128)(2,1)} %param.8) | copy-start | bytes 3145732
  7.2 3.2 copy-start.1
  7.2 165.0 %all-gather.3.cloned.1.call-start = ((), (), s32[]{:S(2)}) async-start(), calls=%async_computation.1 | async-start | bytes 16515072 | tf_op jit(solution)/shard_map/all_gather | solution.py:26
  10.3 192.5 %all-reduce.3.cloned.1.call-start = ((), (), s32[]{:S(2)}) async-start(), calls=%async_computation.3 | async-start | bytes 8388608 | tf_op jit(solution)/shard_map/psum | solution.py:66
  11.7 146.3 %collective-permute-start.1 = (bf16[192,16,256]{2,0,1:T(8,128)(2,1)}, bf16[192,16,256]{2,0,1:T(8,128)(2,1)}, u32[]{:S(2)}, u32[]{:S(2)}) collective-permute-start(bf16[192,16,256]{2,0,1:T(8,128)(2,1)} %bitcast.92), channel_id=1, source_target_pairs={{0,2},{1,3},{2,0},{3,1},{4,6},{5,7},{6,4},{7,5},{8,10},{9,11},{10,... | collective-permute-start | bytes 4718600 | tf_op jit(solution)/shard_map/ppermute | solution.py:8
  15.7 139.6 %collective-permute-start = (bf16[192,16,256]{2,0,1:T(8,128)(2,1)}, bf16[192,16,256]{2,0,1:T(8,128)(2,1)}, u32[]{:S(2)}, u32[]{:S(2)}) collective-permute-start(bf16[192,16,256]{2,0,1:T(8,128)(2,1)} %bitcast.92), channel_id=1, source_target_pairs={{0,1},{1,0},{2,3},{3,2},{4,5},{5,4},{6,7},{7,6},{8,9},{9,8},{10,11... | collective-permute-start | bytes 4718600 | tf_op jit(solution)/shard_map/ppermute | solution.py:8
  94.9 3.4 copy-start.2
  94.9 3.4 copy-start.13
  120.8 187.1 %reduce-scatter.2.cloned.1.call-start = ((), (), s32[]{:S(2)}) async-start(), calls=%async_computation.2 | async-start | bytes 16515072 | tf_op jit(solution)/shard_map/reduce_scatter | solution.py:45
  128.6 1.1 copy-start.4
  131.6 6.0 %copy-start.11 = (bf16[192,4,2,2,256]{4,3,2,1,0:T(2,128)(2,1)S(1)}, bf16[192,4,2,2,256]{4,3,2,1,0:T(2,128)(2,1)}, u32[]{:S(2)}) copy-start(bf16[192,4,2,2,256]{4,3,2,1,0:T(2,128)(2,1)} %reshape_reshape.13) | copy-start | bytes 4718596
  142.0 5.9 %copy-start.5 = (bf16[24,8,16,256]{3,2,1,0:T(8,128)(2,1)S(1)}, bf16[24,8,16,256]{3,2,1,0:T(8,128)(2,1)}, u32[]{:S(2)}) copy-start(bf16[24,8,16,256]{3,2,1,0:T(8,128)(2,1)} %copy-done.4) | copy-start | bytes 4718596
  147.9 1.7 copy-start.12
  147.9 3.0 copy-start.10
  149.6 2.6 copy-start.9
  150.9 2.7 copy-start.8
  152.2 2.6 copy-start.3
  199.9 145.6 %collective-permute-start.3 = (f32[192,16,256]{2,0,1:T(8,128)}, f32[192,16,256]{2,0,1:T(8,128)}, u32[]{:S(2)}, u32[]{:S(2)}) collective-permute-start(f32[192,16,256]{2,0,1:T(8,128)} %get-tuple-element.18), channel_id=1, source_target_pairs={{0,2},{1,3},{2,0},{3,1},{4,6},{5,7},{6,4},{7,5},{8,10},{9,11},{10,... | collective-permute-start | bytes 9437192 | tf_op jit(solution)/shard_map/ppermute | solution.py:8
  200.6 145.0 %collective-permute-start.2 = (f32[192,16,256]{2,0,1:T(8,128)}, f32[192,16,256]{2,0,1:T(8,128)}, u32[]{:S(2)}, u32[]{:S(2)}) collective-permute-start(f32[192,16,256]{2,0,1:T(8,128)} %get-tuple-element.22), channel_id=1, source_target_pairs={{0,1},{1,0},{2,3},{3,2},{4,5},{5,4},{6,7},{7,6},{8,9},{9,8},{10,11... | collective-permute-start | bytes 9437192 | tf_op jit(solution)/shard_map/ppermute | solution.py:8
  337.8 4.0 %copy-start.14 = (bf16[128,4096]{1,0:T(8,128)(2,1)S(1)}, bf16[128,4096]{1,0:T(8,128)(2,1)}, u32[]{:S(2)}) copy-start(bf16[128,4096]{1,0:T(8,128)(2,1)} %param.9) | copy-start | bytes 3145732
  341.8 3.8 %copy-start.6 = (f32[192,8,2,1,256]{4,0,2,1,3:T(8,128)S(1)}, f32[192,8,2,1,256]{4,0,2,1,3:T(8,128)}, u32[]{:S(2)}) copy-start(f32[192,8,2,1,256]{4,0,2,1,3:T(8,128)} %rev.28) | copy-start | bytes 9437188
  355.5 2.8 copy-start.7
  358.4 2.2 copy-start.15
Sparse Core Ops, SparseCore 0:
  10.5 83.6 all-gather.2
  120.9 79.3 all-reduce.2
  204.2 103.6 reduce-scatter.1
